TPU v7x, 32 devices: a whole 2x2x4 slice. The times are simulated.
32 devices in a mesh: sky: 4 (over y, x), depth: 8 (over z, core).
Axes of the slice: x: 2, y: 2, z: 4, core: 2. Of those that a mesh axis runs over, the one named last changes fastest.
Arguments:
- field: float32 [64, 256, 512], P('depth', 'sky'), may hold values from -4 to 4
- momentum: float32 [64, 256, 512], P('depth', 'sky'), may hold values from -4 to 4
- lens_weight: float32 [64], P('depth'), may hold values from 0.1 to 0.4
- source_weight: float32 [64], P('depth'), may hold values from 0.078125 to 0.625
- plane_bin: int32 [64], P('depth'), may hold values from 0 to 9
- observed: float32 [10, 256, 512], P(None, 'sky'), may hold values from -1.5 to 1.5
- noise_inverse: float32 [10], replicated, may hold values from 1 to 4
Outputs:
- field_out: float32 [64, 256, 512], P('depth', 'sky')
- momentum_out: float32 [64, 256, 512], P('depth', 'sky')
All inputs are finite; a program needn't handle non-finite values.
Results may differ from a plain program's by a relative error of at most 0.0003.
Values sent between devices are 32-bit elements; how exact they have to be, the bound alone decides.
A program may use at most 64 MiB of HBM per device.

v0:
```python
import functools
import math

import jax
import jax.numpy as jnp
import numpy as np
from jax import lax
from jax.experimental import pallas as pl
from jax.experimental.pallas import tpu as pltpu
from jax.sharding import PartitionSpec as P

LEAP = 2
amplitude = 3.0
step_size = 0.25
REACH = 6
EDGE = 8
LAG = 2
MESH = pl.DeviceIdType.MESH


def kernel_weights():
    raw = [math.exp(-((offset - 6) ** 2) / 12.5) for offset in range(13)]
    whole = sum(raw)
    return [value / whole for value in raw]


def split_np(values):
    high = values.astype(jnp.bfloat16)
    low = (values - high.astype(np.float64)).astype(jnp.bfloat16)
    return high, low


def smoothing_matrices(rows, cols):
    weights = kernel_weights()

    def band(outs, ins):
        offset = ins[None, :] - outs[:, None] + REACH
        inside = (offset >= 0) & (offset <= 2 * REACH)
        return np.where(inside, np.array(weights)[np.clip(offset, 0, 2 * REACH)], 0.0)

    col_high, col_low = split_np(band(np.arange(cols), np.arange(cols)).T)
    here = np.arange(rows)
    own_high, own_low = split_np(band(here, here))
    around = np.concatenate([np.arange(-EDGE, 0), np.arange(rows, rows + EDGE)])
    far_high, far_low = split_np(band(here, around))
    row_matrix = np.concatenate([own_high, own_high, own_low, far_high, far_high, far_low], axis=1)
    return row_matrix, np.stack([col_high, col_low])


def split(values):
    high = values.astype(jnp.bfloat16)
    low = (values - high.astype(jnp.float32)).astype(jnp.bfloat16)
    return high, low


def kernel(
    ndepth, nsky,
    field_ref, momentum_ref, observed_ref, lens_ref, source_ref, bin_ref, noise_ref, row_ref, col_ref,
    fo, mo,
    density, pulled, stage, edges, table, coupling, mixing, mix, own, chip, rs, prefix, suffix, psend, ssend, scaled,
    edge_send, edge_recv, table_send, table_recv, mix_sem,
    rs_send, rs_recv, p_send, p_recv, s_send, s_recv, ag_send, ag_recv,
):
    planes, rows, cols = fo.shape
    nbins = observed_ref.shape[0]
    blocks = rows // 8
    half = own.shape[2]
    sky = lax.axis_index("sky")
    depth = lax.axis_index("depth")
    chips = ndepth // 2
    place = depth // 2
    core = depth % 2
    partner = place * 2 + 1 - core
    total = planes * ndepth

    barrier = pltpu.get_barrier_semaphore()
    for other in range(1, ndepth):
        peer = lax.rem(depth + other, ndepth)
        pl.semaphore_signal(barrier, inc=1, device_id={"depth": peer}, device_id_type=MESH)

    @pl.when(sky > 0)
    def _():
        pl.semaphore_signal(barrier, inc=1, device_id={"sky": sky - 1}, device_id_type=MESH)

    @pl.when(sky < nsky - 1)
    def _():
        pl.semaphore_signal(barrier, inc=1, device_id={"sky": sky + 1}, device_id_type=MESH)

    fo[...] = field_ref[...]
    mo[...] = momentum_ref[...]
    row_id = lax.broadcasted_iota(jnp.int32, (planes, 128), 0)
    lane_id = lax.broadcasted_iota(jnp.int32, (planes, 128), 1)
    mine = jnp.zeros((planes, 128), jnp.float32)
    lens = jnp.zeros((planes, 128), jnp.float32)
    for q in range(planes):
        mine = jnp.where((row_id == q) & (lane_id == bin_ref[q]), source_ref[q], mine)
        lens = jnp.where(row_id == q, lens_ref[q], lens)
    coupling[...] = mine
    table[depth] = mine

    @pl.when(sky == 0)
    def _():
        edges[:, 0] = jnp.zeros_like(edges[:, 0])

    @pl.when(sky == nsky - 1)
    def _():
        edges[:, 1] = jnp.zeros_like(edges[:, 1])

    @pl.when(place == 0)
    def _():
        prefix[...] = jnp.zeros_like(prefix)

    @pl.when(place == chips - 1)
    def _():
        suffix[...] = jnp.zeros_like(suffix)

    neighbours = jnp.minimum(sky, 1) + jnp.minimum(nsky - 1 - sky, 1)
    pl.semaphore_wait(barrier, ndepth - 1 + neighbours)

    def remote(src, dst, send, recv, where):
        return pltpu.make_async_remote_copy(
            src_ref=src, dst_ref=dst, send_sem=send, recv_sem=recv, device_id=where, device_id_type=MESH
        )

    def edge_copies(src, slot):
        up = remote(
            src.at[:, pl.ds(rows - EDGE, EDGE), :], edges.at[slot, 0],
            edge_send.at[slot, 0], edge_recv.at[slot, 0], {"sky": sky + 1},
        )
        down = remote(
            src.at[:, pl.ds(0, EDGE), :], edges.at[slot, 1],
            edge_send.at[slot, 1], edge_recv.at[slot, 1], {"sky": sky - 1},
        )
        return up, down

    def edge_start(src, slot):
        up, down = edge_copies(src, slot)

        @pl.when(sky < nsky - 1)
        def _():
            up.start()

        @pl.when(sky > 0)
        def _():
            down.start()

    def edge_wait(src, slot):
        up, down = edge_copies(src, slot)

        @pl.when(sky < nsky - 1)
        def _():
            up.wait_send()
            down.wait_recv()

        @pl.when(sky > 0)
        def _():
            down.wait_send()
            up.wait_recv()

    def smooth(src, slot, finish):
        edge_wait(src, slot)

        def row_step(q, carry):
            high, low = split(src[q])
            far_high, far_low = split(jnp.concatenate([edges[slot, 0, q], edges[slot, 1, q]], axis=0))
            tall = jnp.concatenate([high, low, high, far_high, far_low, far_high], axis=0)
            across = jnp.dot(row_ref[...], tall, preferred_element_type=jnp.float32)
            high, low = split(across)
            stage[0, pl.ds(q * rows, rows), :] = high
            stage[1, pl.ds(q * rows, rows), :] = low
            return carry

        lax.fori_loop(0, planes, row_step, 0)
        group = 4 if planes % 4 == 0 else 1

        def col_step(i, carry):
            here = pl.ds(i * (group * rows), group * rows)
            high = stage[0, here, :]
            low = stage[1, here, :]
            result = jnp.dot(high, col_ref[0], preferred_element_type=jnp.float32)
            result = result + jnp.dot(low, col_ref[0], preferred_element_type=jnp.float32)
            result = result + jnp.dot(high, col_ref[1], preferred_element_type=jnp.float32)
            finish(pl.ds(i * group, group), result.reshape(group, rows, cols))
            return carry

        lax.fori_loop(0, planes // group, col_step, 0)

    edge_start(fo, 0)
    table_copies = []
    for other in range(1, ndepth):
        peer = lax.rem(depth + other, ndepth)
        copy = remote(
            coupling, table.at[depth], table_send.at[other - 1], table_recv.at[other - 1], {"depth": peer}
        )
        copy.start()
        table_copies.append(copy)
    for copy in table_copies:
        copy.wait()
    every = table[...].reshape(total, 128)
    near = lax.broadcasted_iota(jnp.int32, (planes, total), 0) + depth * planes
    far = lax.broadcasted_iota(jnp.int32, (planes, total), 1)
    near_r = (near + 1).astype(jnp.float32) / total
    far_r = (far + 1).astype(jnp.float32) / total
    ratio = jnp.where(far > near, 1.0 - near_r / far_r, 0.0)
    mixing[...] = lens * jnp.dot(
        ratio, every, precision=lax.Precision.HIGHEST, preferred_element_type=jnp.float32
    )
    move = pltpu.make_async_copy(mixing, mix, mix_sem)
    move.start()
    move.wait()

    def gradient_step(t, carry):
        slot = 2 * t

        def keep_density(which, value):
            density[which] = jnp.exp(amplitude * value)

        smooth(fo, slot, keep_density)

        def rs_copy(g):
            return remote(
                own.at[g, 1 - core], rs.at[t, g], rs_send.at[t, g], rs_recv.at[t, g], {"depth": partner}
            )

        def p_copy(g):
            return remote(
                psend.at[g], prefix.at[t, g], p_send.at[t, g], p_recv.at[t, g], {"depth": depth + 2}
            )

        def s_copy(g):
            return remote(
                ssend.at[g], suffix.at[t, g], s_send.at[t, g], s_recv.at[t, g], {"depth": depth - 2}
            )

        def ag_copy(g):
            return remote(
                scaled.at[t, g, core], scaled.at[t, g, core], ag_send.at[t, g], ag_recv.at[t, g],
                {"depth": partner},
            )

        def ag_wait(g):
            return remote(
                scaled.at[t, g, core], scaled.at[t, g, 1 - core], ag_send.at[t, g], ag_recv.at[t, g],
                {"depth": partner},
            )

        def partial_step(g, carry):
            here = pl.ds(pl.multiple_of(g * 8, 8), 8)
            excess = [density[q, here, :] - 1.0 for q in range(planes)]
            for b in range(2 * half):
                if b < nbins:
                    value = mix[0, b] * excess[0]
                    for q in range(1, planes):
                        value = value + mix[q, b] * excess[q]
                else:
                    value = jnp.zeros_like(excess[0])
                own[g, b // half, b % half] = value
            rs_copy(g).start()
            return carry

        lax.fori_loop(0, blocks, partial_step, 0)

        def ring_step(i, carry):
            @pl.when(i < blocks)
            def _():
                rs_copy(i).wait_recv()
                chip[i] = own[i, core] + rs[t, i]

            j = i - LAG * place

            @pl.when((j >= 0) & (j < blocks))
            def _():
                @pl.when(place > 0)
                def _():
                    p_copy(j).wait_recv()

                @pl.when(place < chips - 1)
                def _():
                    psend[j] = prefix[t, j] + chip[j]
                    p_copy(j).start()

            k = i - LAG * (chips - 1 - place)

            @pl.when((k >= 0) & (k < blocks))
            def _():
                @pl.when(place < chips - 1)
                def _():
                    s_copy(k).wait_recv()

                @pl.when(place > 0)
                def _():
                    ssend[k] = suffix[t, k] + chip[k]
                    s_copy(k).start()

            m = i - LAG * jnp.maximum(place, chips - 1 - place)

            @pl.when((m >= 0) & (m < blocks))
            def _():
                here = pl.ds(pl.multiple_of(m * 8, 8), 8)
                for b in range(half):
                    at = jnp.minimum(core * half + b, nbins - 1)
                    whole = prefix[t, m, b] + chip[m, b] + suffix[t, m, b]
                    scaled[t, m, core, b] = noise_ref[at] * (whole - observed_ref[at, here, :])
                ag_copy(m).start()

            return carry

        lax.fori_loop(0, blocks + LAG * (chips - 1), ring_step, 0)

        def pull_step(g, carry):
            ag_wait(g).wait_recv()
            here = pl.ds(pl.multiple_of(g * 8, 8), 8)
            maps = [scaled[t, g, b // half, b % half] for b in range(nbins)]
            for q in range(planes):
                value = mix[q, 0] * maps[0]
                for b in range(1, nbins):
                    value = value + mix[q, b] * maps[b]
                pulled[q, here, :] = value * density[q, here, :]
            return carry

        lax.fori_loop(0, blocks, pull_step, 0)
        edge_start(pulled, slot + 1)

        def drain(g, carry):
            rs_copy(g).wait_send()
            ag_copy(g).wait_send()

            @pl.when(place < chips - 1)
            def _():
                p_copy(g).wait_send()

            @pl.when(place > 0)
            def _():
                s_copy(g).wait_send()

            return carry

        lax.fori_loop(0, blocks, drain, 0)
        last = t == LEAP
        factor = jnp.where((t == 0) | last, 0.5 * step_size, step_size)
        drift = jnp.where(last, 0.0, step_size)

        def kick(which, value):
            position = fo[which]
            moving = mo[which] - factor * (position + amplitude * value)
            mo[which] = moving
            fo[which] = position + drift * moving

        smooth(pulled, slot + 1, kick)

        @pl.when(t < LEAP)
        def _():
            edge_start(fo, slot + 2)

        return carry

    lax.fori_loop(0, LEAP + 1, gradient_step, 0)


def body(ndepth, nsky, field, momentum, lens_weight, source_weight, plane_bin, observed, noise_inverse):
    planes, rows, cols = field.shape
    nbins = observed.shape[0]
    half = (nbins + 1) // 2
    blocks = rows // 8
    grads = LEAP + 1
    row_matrix, col_matrix = smoothing_matrices(rows, cols)
    f32 = jnp.float32
    vmem = pl.BlockSpec(memory_space=pltpu.VMEM)
    smem = pl.BlockSpec(memory_space=pltpu.SMEM)
    dma = pltpu.SemaphoreType.DMA
    piece = (half, 8, cols)
    return pl.pallas_call(
        functools.partial(kernel, ndepth, nsky),
        out_shape=(jax.ShapeDtypeStruct(field.shape, f32),) * 2,
        in_specs=[vmem, vmem, vmem, smem, smem, smem, smem, vmem, vmem],
        out_specs=(vmem, vmem),
        scratch_shapes=[
            pltpu.VMEM((planes, rows, cols), f32),
            pltpu.VMEM((planes, rows, cols), f32),
            pltpu.VMEM((2, planes * rows, cols), jnp.bfloat16),
            pltpu.VMEM((2 * grads, 2, planes, EDGE, cols), f32),
            pltpu.VMEM((ndepth, planes, 128), f32),
            pltpu.VMEM((planes, 128), f32),
            pltpu.VMEM((planes, 128), f32),
            pltpu.SMEM((planes, 128), f32),
            pltpu.VMEM((blocks, 2) + piece, f32),
            pltpu.VMEM((blocks,) + piece, f32),
            pltpu.VMEM((grads, blocks) + piece, f32),
            pltpu.VMEM((grads, blocks) + piece, f32),
            pltpu.VMEM((grads, blocks) + piece, f32),
            pltpu.VMEM((blocks,) + piece, f32),
            pltpu.VMEM((blocks,) + piece, f32),
            pltpu.VMEM((grads, blocks, 2) + piece, f32),
            dma((2 * grads, 2)), dma((2 * grads, 2)),
            dma((ndepth - 1,)), dma((ndepth - 1,)), dma,
        ] + [dma((grads, blocks))] * 8,
        compiler_params=pltpu.CompilerParams(
            collective_id=0, has_side_effects=True, vmem_limit_bytes=56 * 1024 * 1024
        ),
        name="leapfrog",
    )(
        field, momentum, observed, lens_weight, source_weight, plane_bin, noise_inverse,
        jnp.asarray(row_matrix), jnp.asarray(col_matrix),
    )


def solution(mesh):
    return jax.shard_map(
        functools.partial(body, mesh.shape["depth"], mesh.shape["sky"]),
        mesh=mesh,
        in_specs=(
            P("depth", "sky", None),
            P("depth", "sky", None),
            P("depth"),
            P("depth"),
            P("depth"),
            P(None, "sky", None),
            P(),
        ),
        out_specs=(P("depth", "sky", None), P("depth", "sky", None)),
        check_vma=False,
    )
```

profile of v0, /device:TPU:0, one launch (start us, length us, event | category | flops | bytes accessed | tf_op | source)
XLA Modules:
  0.0 151.0 jit_solution(9528166401622201752)
XLA Ops:
  0.6 147.0 %leapfrog.1 = (f32[8,64,512]{2,1,0:T(8,128)}, f32[8,64,512]{2,1,0:T(8,128)}) custom-call(f32[8,64,512]{2,1,0:T(8,128)} %field_ref.1, f32[8,64,512]{2,1,0:T(8,128)} %momentum_ref.1, f32[10,64,512]{2,1,0:T(8,128)} %observed_ref.1, f32[8]{0:T(128)} %lens_ref.1, f32[8]{0:T(128)} %source_ref.1, s32[8]{0:T(128)} %bin_ref.1, f32[10]{0:T(128)} %noise_ref.1, ...), custom_call_target="tpu_custom_call" | custom-call | tf_op jit(solution)/shard_map/leapfrog/pallas_call | solution.py:372
  147.6 0.0 copy-start
  147.7 2.4 %copy.13 = f32[8,64,512]{2,1,0:T(8,128)} copy(f32[8,64,512]{2,1,0:T(8,128)} %get-tuple-element.4) | data formatting | bytes 2097152
  150.0 0.0 copy-done
  150.0 1.0 copy.14
Async XLA Ops:
  147.6 2.4 %copy-start = (f32[8,64,512]{2,1,0:T(8,128)S(1)}, f32[8,64,512]{2,1,0:T(8,128)}, u32[]{:S(2)}) copy-start(f32[8,64,512]{2,1,0:T(8,128)} %get-tuple-element.5) | copy-start | bytes 3145732
where the time goes:
time: 151 us
  Pallas kernels  147 us (97%)
  local copies, waits for them, and re-layouts  3.32 us (2%)
    pallas_call x1, Pallas kernels, body(): pl.pallas_call(functools.partial(kernel, ndepth, nsky), out_shape=(jax.Sh...  147 us
    unnamed x4, local copies, waits for them, and re-layouts  3.32 us

commit v1 on v0

v1 whole, which is shorter than its diff:
```python
import functools
import math

import jax
import jax.numpy as jnp
import numpy as np
from jax import lax
from jax.experimental import pallas as pl
from jax.experimental.pallas import tpu as pltpu
from jax.sharding import PartitionSpec as P

LEAP = 2
amplitude = 3.0
step_size = 0.25
REACH = 6
GROUP = 4
EDGE = 8
LAG = 4
PAIR_LAG = 2
MESH = pl.DeviceIdType.MESH


def kernel_weights():
    raw = [math.exp(-((offset - 6) ** 2) / 12.5) for offset in range(13)]
    whole = sum(raw)
    return [value / whole for value in raw]


def split_np(values):
    high = values.astype(jnp.bfloat16)
    low = (values - high.astype(np.float64)).astype(jnp.bfloat16)
    return high, low


def smoothing_matrices(rows, cols):
    weights = kernel_weights()

    def band(outs, ins):
        offset = ins[None, :] - outs[:, None] + REACH
        inside = (offset >= 0) & (offset <= 2 * REACH)
        return np.where(inside, np.array(weights)[np.clip(offset, 0, 2 * REACH)], 0.0)

    col_high, col_low = split_np(band(np.arange(cols), np.arange(cols)).T)
    here = np.arange(rows)
    own_high, own_low = split_np(band(here, here))
    around = np.concatenate([np.arange(-EDGE, 0), np.arange(rows, rows + EDGE)])
    ends = np.concatenate([np.arange(EDGE), np.arange(rows - EDGE, rows)])
    far_high, far_low = split_np(band(ends, around))
    row_matrix = np.concatenate([own_high, own_high, own_low], axis=1)
    far_matrix = np.concatenate([far_high, far_high, far_low], axis=1)
    return row_matrix, far_matrix, np.stack([col_high, col_low])


def split(values):
    high = values.astype(jnp.bfloat16)
    low = (values - high.astype(jnp.float32)).astype(jnp.bfloat16)
    return high, low


def kernel(
    ndepth, nsky,
    field_ref, momentum_ref, observed_hbm, lens_ref, source_ref, bin_ref, noise_ref, row_ref, far_ref, col_ref,
    fo, mo,
    observed_ref, density, pulled, stage, edges, table, coupling, mixing, mix, own, chip, rs, prefix, suffix, psend, ssend, scaled,
    load_sem, edge_send, edge_recv, table_send, table_recv, mix_sem,
    rs_send, rs_recv, p_send, p_recv, s_send, s_recv, ag_send, ag_recv,
):
    planes, rows, cols = fo.shape
    nbins = observed_ref.shape[0]
    pieces = own.shape[0]
    half = own.shape[2]
    width = own.shape[4]
    across_count = cols // width
    blocks = rows // 8
    group = GROUP if planes % GROUP == 0 else 1
    groups = planes // group
    loads = [
        pltpu.make_async_copy(field_ref, fo, load_sem.at[0]),
        pltpu.make_async_copy(momentum_ref, mo, load_sem.at[1]),
        pltpu.make_async_copy(observed_hbm, observed_ref, load_sem.at[2]),
    ]
    for load in loads:
        load.start()
    sky = lax.axis_index("sky")
    depth = lax.axis_index("depth")
    chips = ndepth // 2
    place = depth // 2
    core = depth % 2
    partner = place * 2 + 1 - core
    total = planes * ndepth

    barrier = pltpu.get_barrier_semaphore()
    for other in range(1, ndepth):
        peer = lax.rem(depth + other, ndepth)
        pl.semaphore_signal(barrier, inc=1, device_id={"depth": peer}, device_id_type=MESH)

    @pl.when(sky > 0)
    def _():
        pl.semaphore_signal(barrier, inc=1, device_id={"sky": sky - 1}, device_id_type=MESH)

    @pl.when(sky < nsky - 1)
    def _():
        pl.semaphore_signal(barrier, inc=1, device_id={"sky": sky + 1}, device_id_type=MESH)

    row_id = lax.broadcasted_iota(jnp.int32, (planes, 128), 0)
    lane_id = lax.broadcasted_iota(jnp.int32, (planes, 128), 1)
    mine = jnp.zeros((planes, 128), jnp.float32)
    lens = jnp.zeros((planes, 128), jnp.float32)
    for q in range(planes):
        mine = jnp.where((row_id == q) & (lane_id == bin_ref[q]), source_ref[q], mine)
        lens = jnp.where(row_id == q, lens_ref[q], lens)
    coupling[...] = mine
    table[depth] = mine

    for slot in range(edges.shape[0]):
        for q in range(planes):
            edges[slot, 0, q, : EDGE - REACH, :] = jnp.zeros((EDGE - REACH, cols), jnp.float32)
            edges[slot, 1, q, REACH:, :] = jnp.zeros((EDGE - REACH, cols), jnp.float32)

    @pl.when(sky == 0)
    def _():
        edges[:, 0] = jnp.zeros_like(edges[:, 0])

    @pl.when(sky == nsky - 1)
    def _():
        edges[:, 1] = jnp.zeros_like(edges[:, 1])

    @pl.when(place == 0)
    def _():
        prefix[...] = jnp.zeros_like(prefix)

    @pl.when(place == chips - 1)
    def _():
        suffix[...] = jnp.zeros_like(suffix)

    neighbours = jnp.minimum(sky, 1) + jnp.minimum(nsky - 1 - sky, 1)
    pl.semaphore_wait(barrier, ndepth - 1 + neighbours)

    def remote(src, dst, send, recv, where):
        return pltpu.make_async_remote_copy(
            src_ref=src, dst_ref=dst, send_sem=send, recv_sem=recv, device_id=where, device_id_type=MESH
        )

    def edge_copies(src, slot, i):
        these = pl.ds(i * group, group)
        up = remote(
            src.at[these, pl.ds(rows - REACH, REACH), :], edges.at[slot, 0, these, pl.ds(EDGE - REACH, REACH), :],
            edge_send.at[slot, 0, i], edge_recv.at[slot, 0, i], {"sky": sky + 1},
        )
        down = remote(
            src.at[these, pl.ds(0, REACH), :], edges.at[slot, 1, these, pl.ds(0, REACH), :],
            edge_send.at[slot, 1, i], edge_recv.at[slot, 1, i], {"sky": sky - 1},
        )
        return up, down

    def edge_start(src, slot, i):
        up, down = edge_copies(src, slot, i)

        @pl.when(sky < nsky - 1)
        def _():
            up.start()

        @pl.when(sky > 0)
        def _():
            down.start()

    def edge_wait(src, slot, i):
        up, down = edge_copies(src, slot, i)

        @pl.when(sky < nsky - 1)
        def _():
            up.wait_send()
            down.wait_recv()

        @pl.when(sky > 0)
        def _():
            down.wait_send()
            up.wait_recv()

    def smooth(src, slot, finish):
        def row_step(q, carry):
            high, low = split(src[q])
            tall = jnp.concatenate([high, low, high], axis=0)
            stage[q] = jnp.dot(row_ref[...], tall, preferred_element_type=jnp.float32)
            return carry

        lax.fori_loop(0, planes, row_step, 0, unroll=4 if planes % 4 == 0 else 1)

        def col_step(i, carry):
            edge_wait(src, slot, i)
            for inner in range(group):
                q = i * group + inner
                high, low = split(jnp.concatenate([edges[slot, 0, q], edges[slot, 1, q]], axis=0))
                tall = jnp.concatenate([high, low, high], axis=0)
                far = jnp.dot(far_ref[...], tall, preferred_element_type=jnp.float32)
                stage[q, pl.ds(0, EDGE), :] = stage[q, pl.ds(0, EDGE), :] + far[:EDGE]
                stage[q, pl.ds(rows - EDGE, EDGE), :] = stage[q, pl.ds(rows - EDGE, EDGE), :] + far[EDGE:]
            these = pl.ds(i * group, group)
            high, low = split(stage[these].reshape(group * rows, cols))
            result = jnp.dot(high, col_ref[0], preferred_element_type=jnp.float32)
            result = result + jnp.dot(low, col_ref[0], preferred_element_type=jnp.float32)
            result = result + jnp.dot(high, col_ref[1], preferred_element_type=jnp.float32)
            finish(i, these, result.reshape(group, rows, cols))
            return carry

        lax.fori_loop(0, groups, col_step, 0)

    loads[0].wait()
    for i in range(groups):
        edge_start(fo, 0, i)
    table_copies = []
    for other in range(1, ndepth):
        peer = lax.rem(depth + other, ndepth)
        copy = remote(
            coupling, table.at[depth], table_send.at[other - 1], table_recv.at[other - 1], {"depth": peer}
        )
        copy.start()
        table_copies.append(copy)
    for copy in table_copies:
        copy.wait()
    every = table[...].reshape(total, 128)
    near = lax.broadcasted_iota(jnp.int32, (planes, total), 0) + depth * planes
    far = lax.broadcasted_iota(jnp.int32, (planes, total), 1)
    near_r = (near + 1).astype(jnp.float32) / total
    far_r = (far + 1).astype(jnp.float32) / total
    ratio = jnp.where(far > near, 1.0 - near_r / far_r, 0.0)
    mixing[...] = lens * jnp.dot(
        ratio, every, precision=lax.Precision.HIGHEST, preferred_element_type=jnp.float32
    )
    move = pltpu.make_async_copy(mixing, mix, mix_sem)
    move.start()
    move.wait()
    loads[1].wait()
    loads[2].wait()

    def gradient_step(t, carry):
        slot = 2 * t

        def keep_density(i, which, value):
            density[which] = jnp.exp(amplitude * value)

        smooth(fo, slot, keep_density)

        def rs_copy(g):
            return remote(
                own.at[g, 1 - core], rs.at[t, g], rs_send.at[t, g], rs_recv.at[t, g], {"depth": partner}
            )

        def p_copy(g):
            return remote(
                psend.at[g], prefix.at[t, g], p_send.at[t, g], p_recv.at[t, g], {"depth": depth + 2}
            )

        def s_copy(g):
            return remote(
                ssend.at[g], suffix.at[t, g], s_send.at[t, g], s_recv.at[t, g], {"depth": depth - 2}
            )

        def ag_copy(g):
            return remote(
                scaled.at[t, g, core], scaled.at[t, g, core], ag_send.at[t, g], ag_recv.at[t, g],
                {"depth": partner},
            )

        def ag_wait(g):
            return remote(
                scaled.at[t, g, core], scaled.at[t, g, 1 - core], ag_send.at[t, g], ag_recv.at[t, g],
                {"depth": partner},
            )

        def window(g):
            block = g // across_count
            block = jnp.where(block == 0, 0, jnp.where(block == 1, blocks - 1, block - 1))
            return (
                pl.ds(pl.multiple_of(block * 8, 8), 8),
                pl.ds(pl.multiple_of((g % across_count) * width, width), width),
            )

        def sum_step(i, carry):
            @pl.when(i < pieces)
            def _():
                here, there = window(i)
                excess = [density[q, here, there] - 1.0 for q in range(planes)]
                for b in range(2 * half):
                    if b < nbins:
                        value = mix[0, b] * excess[0]
                        for q in range(1, planes):
                            value = value + mix[q, b] * excess[q]
                    else:
                        value = jnp.zeros_like(excess[0])
                    own[i, b // half, b % half] = value
                rs_copy(i).start()

            base = i - PAIR_LAG

            @pl.when((base >= 0) & (base < pieces))
            def _():
                rs_copy(base).wait_recv()
                chip[base] = own[base, core] + rs[t, base]

            j = base - LAG * place

            @pl.when((j >= 0) & (j < pieces))
            def _():
                @pl.when(place > 0)
                def _():
                    p_copy(j).wait_recv()

                @pl.when(place < chips - 1)
                def _():
                    psend[j] = prefix[t, j] + chip[j]
                    p_copy(j).start()

            k = base - LAG * (chips - 1 - place)

            @pl.when((k >= 0) & (k < pieces))
            def _():
                @pl.when(place < chips - 1)
                def _():
                    s_copy(k).wait_recv()

                @pl.when(place > 0)
                def _():
                    ssend[k] = suffix[t, k] + chip[k]
                    s_copy(k).start()

            m = base - LAG * jnp.maximum(place, chips - 1 - place)

            @pl.when((m >= 0) & (m < pieces))
            def _():
                here, there = window(m)
                for b in range(half):
                    at = jnp.minimum(core * half + b, nbins - 1)
                    whole = prefix[t, m, b] + chip[m, b] + suffix[t, m, b]
                    scaled[t, m, core, b] = noise_ref[at] * (whole - observed_ref[at, here, there])
                ag_copy(m).start()

            r = m - PAIR_LAG

            @pl.when((r >= 0) & (r < pieces))
            def _():
                ag_wait(r).wait_recv()
                here, there = window(r)
                maps = [scaled[t, r, b // half, b % half] for b in range(nbins)]
                for q in range(planes):
                    value = mix[q, 0] * maps[0]
                    for b in range(1, nbins):
                        value = value + mix[q, b] * maps[b]
                    pulled[q, here, there] = value * density[q, here, there]

            @pl.when(r == edges_ready)
            def _():
                for group_at in range(groups):
                    edge_start(pulled, slot + 1, group_at)

            return carry

        edges_ready = min(2, blocks) * across_count - 1
        steps = pieces + 2 * PAIR_LAG + LAG * (chips - 1)
        lax.fori_loop(0, steps, sum_step, 0)

        def drain(g, carry):
            rs_copy(g).wait_send()
            ag_copy(g).wait_send()

            @pl.when(place < chips - 1)
            def _():
                p_copy(g).wait_send()

            @pl.when(place > 0)
            def _():
                s_copy(g).wait_send()

            return carry

        lax.fori_loop(0, pieces, drain, 0)
        last = t == LEAP
        factor = jnp.where((t == 0) | last, 0.5 * step_size, step_size)
        drift = jnp.where(last, 0.0, step_size)

        def kick(i, which, value):
            position = fo[which]
            moving = mo[which] - factor * (position + amplitude * value)
            mo[which] = moving
            fo[which] = position + drift * moving

            @pl.when(t < LEAP)
            def _():
                edge_start(fo, slot + 2, i)

        smooth(pulled, slot + 1, kick)
        return carry

    lax.fori_loop(0, LEAP + 1, gradient_step, 0)


def body(ndepth, nsky, field, momentum, lens_weight, source_weight, plane_bin, observed, noise_inverse):
    planes, rows, cols = field.shape
    nbins = observed.shape[0]
    half = (nbins + 1) // 2
    width = cols // 2 if cols % 256 == 0 else cols
    pieces = rows // 8 * (cols // width)
    groups = planes // GROUP if planes % GROUP == 0 else planes
    grads = LEAP + 1
    row_matrix, far_matrix, col_matrix = smoothing_matrices(rows, cols)
    f32 = jnp.float32
    vmem = pl.BlockSpec(memory_space=pltpu.VMEM)
    smem = pl.BlockSpec(memory_space=pltpu.SMEM)
    dma = pltpu.SemaphoreType.DMA
    piece = (half, 8, width)
    hbm = pl.BlockSpec(memory_space=pl.ANY)
    return pl.pallas_call(
        functools.partial(kernel, ndepth, nsky),
        out_shape=(jax.ShapeDtypeStruct(field.shape, f32),) * 2,
        in_specs=[hbm, hbm, hbm, smem, smem, smem, smem, vmem, vmem, vmem],
        out_specs=(vmem, vmem),
        scratch_shapes=[
            pltpu.VMEM(observed.shape, f32),
            pltpu.VMEM((planes, rows, cols), f32),
            pltpu.VMEM((planes, rows, cols), f32),
            pltpu.VMEM((planes, rows, cols), f32),
            pltpu.VMEM((2 * grads, 2, planes, EDGE, cols), f32),
            pltpu.VMEM((ndepth, planes, 128), f32),
            pltpu.VMEM((planes, 128), f32),
            pltpu.VMEM((planes, 128), f32),
            pltpu.SMEM((planes, 128), f32),
            pltpu.VMEM((pieces, 2) + piece, f32),
            pltpu.VMEM((pieces,) + piece, f32),
            pltpu.VMEM((grads, pieces) + piece, f32),
            pltpu.VMEM((grads, pieces) + piece, f32),
            pltpu.VMEM((grads, pieces) + piece, f32),
            pltpu.VMEM((pieces,) + piece, f32),
            pltpu.VMEM((pieces,) + piece, f32),
            pltpu.VMEM((grads, pieces, 2) + piece, f32),
            dma((3,)), dma((2 * grads, 2, groups)), dma((2 * grads, 2, groups)),
            dma((ndepth - 1,)), dma((ndepth - 1,)), dma,
        ] + [dma((grads, pieces))] * 8,
        compiler_params=pltpu.CompilerParams(
            collective_id=0, has_side_effects=True, vmem_limit_bytes=56 * 1024 * 1024
        ),
        name="leapfrog",
    )(
        field, momentum, observed, lens_weight, source_weight, plane_bin, noise_inverse,
        jnp.asarray(row_matrix), jnp.asarray(far_matrix), jnp.asarray(col_matrix),
    )


def solution(mesh):
    return jax.shard_map(
        functools.partial(body, mesh.shape["depth"], mesh.shape["sky"]),
        mesh=mesh,
        in_specs=(
            P("depth", "sky", None),
            P("depth", "sky", None),
            P("depth"),
            P("depth"),
            P("depth"),
            P(None, "sky", None),
            P(),
        ),
        out_specs=(P("depth", "sky", None), P("depth", "sky", None)),
        check_vma=False,
    )
```

time: 151 us -> 117 us (0.77)
  Pallas kernels: 147 us -> 113 us
    pallas_call x1, Pallas kernels: 147 us -> 113 us  [body(): pl.pallas_call(functools.partial(kernel, ndepth, nsky), out_shape=(jax.Sh...]
where the time goes in v1:
time: 117 us
  Pallas kernels  113 us (97%)
  local copies, waits for them, and re-layouts  3.32 us (3%)
    pallas_call x1, Pallas kernels, body(): pl.pallas_call(functools.partial(kernel, ndepth, nsky), out_shape=(jax.Sh...  113 us
    unnamed x4, local copies, waits for them, and re-layouts  3.32 us

profile of v1, /device:TPU:0, one launch (start us, length us, event | category | flops | bytes accessed | tf_op | source)
XLA Modules:
  0.0 116.6 jit_solution(3332717103987720957)
XLA Ops:
  0.6 112.6 %leapfrog.1 = (f32[8,64,512]{2,1,0:T(8,128)}, f32[8,64,512]{2,1,0:T(8,128)}) custom-call(f32[8,64,512]{2,1,0:T(8,128)} %field_ref.1, f32[8,64,512]{2,1,0:T(8,128)} %momentum_ref.1, f32[10,64,512]{2,1,0:T(8,128)} %observed_hbm.1, f32[8]{0:T(128)} %lens_ref.1, f32[8]{0:T(128)} %source_ref.1, s32[8]{0:T(128)} %bin_ref.1, f32[10]{0:T(128)} %noise_ref.1, ...), custom_call_target="tpu_custom_call" | custom-call | tf_op jit(solution)/shard_map/leapfrog/pallas_call | solution.py:412
  113.3 0.0 copy-start
  113.3 2.4 %copy.14 = f32[8,64,512]{2,1,0:T(8,128)} copy(f32[8,64,512]{2,1,0:T(8,128)} %get-tuple-element.4) | data formatting | bytes 2097152
  115.6 0.0 copy-done
  115.7 1.0 copy.15
Async XLA Ops:
  113.3 2.4 %copy-start = (f32[8,64,512]{2,1,0:T(8,128)S(1)}, f32[8,64,512]{2,1,0:T(8,128)}, u32[]{:S(2)}) copy-start(f32[8,64,512]{2,1,0:T(8,128)} %get-tuple-element.5) | copy-start | bytes 3145732
